TPU v7x, 32 devices: a whole 2x2x4 slice. The times are simulated.
32 devices in a mesh: groups: 2 (over y), shot: 4 (over z), slab: 4 (over x, core).
Axes of the slice: x: 2, y: 2, z: 4, core: 2. Of those that a mesh axis runs over, the one named last changes fastest.
Arguments:
- model: float32 [64, 64, 128], P(('groups', 'slab')), parts along dimension 0, may hold values from 0.05 to 0.3
- fwd_now: float32 [8, 32, 64, 128], P(('groups', 'shot'), 'slab'), parts along dimension 0, may hold values from -6 to 6
- fwd_next: float32 [8, 32, 64, 128], P(('groups', 'shot'), 'slab'), parts along dimension 0, may hold values from -6 to 6
- adj_now: float32 [8, 32, 64, 128], P(('groups', 'shot'), 'slab'), parts along dimension 0, may hold values from -6 to 6
- adj_next: float32 [8, 32, 64, 128], P(('groups', 'shot'), 'slab'), parts along dimension 0, may hold values from -6 to 6
- wavelet: float32 [8, 8], P(('groups', 'shot')), parts along dimension 0, may hold values from -16 to 16
- misfit: float32 [8, 8, 128], P(('groups', 'shot')), parts along dimension 0, may hold values from -6 to 6
- src_index: int32 [8], P(('groups', 'shot')), parts along dimension 0, may hold values from 0 to 262143
- rec_index: int32 [8, 128], P(('groups', 'shot')), parts along dimension 0, may hold values from 0 to 262143
Outputs:
- new_model: float32 [64, 64, 128], P(('groups', 'slab')), parts along dimension 0
- stepped: float32 [8, 32, 64, 128], P(('groups', 'shot'), 'slab'), parts along dimension 0
- adjoint_start: float32 [8, 32, 64, 128], P(('groups', 'shot'), 'slab'), parts along dimension 0
There are 2 independent parts, one for each index of `groups`. A program takes and returns all parts, laid end to end along the dimension named above; each array names one. Nothing has to cross between parts.
All inputs are finite; a program needn't handle non-finite values. Where the computation divides by a largest or mean magnitude, that divisor is 1e-20 or more.
Results may differ from a plain program's by a relative error of at most 0.00002.
Values sent between devices are 32-bit elements; how exact they have to be, the bound alone decides.
No kernel may reach another device: no remote copies, remote signals or barrier semaphores. Data moves between devices by JAX's collectives and lax.ppermute only.
A program may use at most 64 MiB of HBM per device.

v0:
```python
import jax
import jax.numpy as jnp
from jax import lax
from jax.sharding import PartitionSpec as P

ITERS = 8


def extended(block, sides, width):
    for axis, dim in sides:
        count = lax.axis_size(axis)
        forward = [(i, i + 1) for i in range(count - 1)]
        backward = [(target, source) for source, target in forward]
        low = lax.ppermute(
            lax.slice_in_dim(block, block.shape[dim] - width, None, axis=dim), axis, forward
        )
        high = lax.ppermute(lax.slice_in_dim(block, 0, width, axis=dim), axis, backward)
        block = jnp.concatenate([low, block, high], axis=dim)
    return block


def local_laplace(padded):
    full = jnp.pad(padded, ((0, 0), (0, 0), (1, 1), (1, 1)))
    center = full[:, 1:-1, 1:-1, 1:-1]
    beside = full[:, 2:, 1:-1, 1:-1] + full[:, :-2, 1:-1, 1:-1]
    beside = beside + full[:, 1:-1, 2:, 1:-1] + full[:, 1:-1, :-2, 1:-1]
    beside = beside + full[:, 1:-1, 1:-1, 2:] + full[:, 1:-1, 1:-1, :-2]
    return beside - 6.0 * center


def inject(field, index, values, offset):
    shots = field.shape[0]
    cells = field.shape[1] * field.shape[2] * field.shape[3]
    flat = field.reshape(shots, -1)
    local = index - offset
    valid = (local >= 0) & (local < cells)
    local = jnp.clip(local, 0, cells - 1)
    rows = jnp.arange(shots, dtype=jnp.int32).reshape((shots,) + (1,) * (index.ndim - 1))
    rows = jnp.broadcast_to(rows, index.shape)
    flat = flat.at[rows, local].add(jnp.where(valid, values, 0.0))
    return flat.reshape(field.shape)


def update(model, gradient, peak):
    return jnp.clip(model - 0.1 * gradient / (peak + 1e-06), 0.05, 0.3)


def per_device(model, fwd_now, fwd_next, adj_now, adj_next, wavelet, misfit, src_index, rec_index):
    shots = fwd_now.shape[0]
    depth, width, length = model.shape
    offset = lax.axis_index("slab") * (depth * width * length)
    wave, wave_later = (fwd_now, fwd_next)
    adjoint, adjoint_later = (adj_now, adj_next)
    image = jnp.zeros_like(fwd_now)
    for step in range(ITERS):
        stacked = jnp.concatenate([wave, adjoint], axis=0)
        padded = extended(stacked, (("slab", 1),), 1)
        laps = local_laplace(padded)
        lap_wave = laps[:shots]
        lap_adjoint = laps[shots:]
        image = image + adjoint * lap_wave
        wave_prior = 2.0 * wave - wave_later + model[None] * lap_wave
        wave_prior = inject(wave_prior, src_index, wavelet[:, step], offset)
        adjoint_prior = 2.0 * adjoint - adjoint_later + model[None] * lap_adjoint
        adjoint_prior = inject(adjoint_prior, rec_index, misfit[:, step, :], offset)
        wave_later, wave = (wave, wave_prior)
        adjoint_later, adjoint = (adjoint, adjoint_prior)
    local_image = jnp.sum(image, axis=0)
    gradient = lax.psum(local_image, "shot")
    peak = lax.pmax(jnp.max(jnp.abs(gradient)), "slab")
    new_model = update(model, gradient, peak)
    padded_wave = extended(wave, (("slab", 1),), 1)
    stepped = 2.0 * wave - wave_later + new_model[None] * local_laplace(padded_wave)
    return (new_model, stepped, adjoint)


def solution(mesh):
    in_specs = (
        P(("groups", "slab"), None, None),
        P(("groups", "shot"), "slab", None, None),
        P(("groups", "shot"), "slab", None, None),
        P(("groups", "shot"), "slab", None, None),
        P(("groups", "shot"), "slab", None, None),
        P(("groups", "shot"), None),
        P(("groups", "shot"), None, None),
        P(("groups", "shot")),
        P(("groups", "shot"), None),
    )
    out_specs = (
        P(("groups", "slab"), None, None),
        P(("groups", "shot"), "slab", None, None),
        P(("groups", "shot"), "slab", None, None),
    )
    return jax.shard_map(
        per_device, mesh=mesh, in_specs=in_specs, out_specs=out_specs, check_vma=False
    )
```

profile of v0, /device:TPU:0, one launch (start us, length us, event | category | flops | bytes accessed | tf_op | source)
XLA Modules:
  0.0 169.2 jit_solution(971231168128775817)
XLA Ops:
  7.2 1.0 constant_dynamic-update-slice_fusion.1
  8.2 1.0 constant_dynamic-update-slice_fusion
  9.2 2.4 %collective-permute-start.1 = (f32[2,1,64,128]{3,2,1,0:T(8,128)S(1)}, f32[2,1,64,128]{3,2,1,0:T(8,128)S(1)}, u32[]{:S(2)}, u32[]{:S(2)}) collective-permute-start(f32[2,1,64,128]{3,2,1,0:T(8,128)S(1)} %get-tuple-element.133), channel_id=1, source_target_pairs={{0,1},{1,2},{2,3},{4,5},{5,6},{6,7},{8,9},{9,10},{10,11},{12,13},{... | collective-permute-start | bytes 196616 | tf_op jit(solution)/shard_map/ppermute | solution.py:14
  11.6 1.3 collective-permute-start
  13.5 0.7 fusion.64
  14.2 0.7 fusion.65
  14.9 0.9 fusion.66
  15.9 1.6 fusion.75
  18.2 0.7 and_reduce_fusion
  18.9 0.4 select_maximum_fusion.21
  19.4 0.5 fusion.27
  20.8 0.7 fusion.76
  23.4 1.4 scatter_fusion
  24.8 5.1 %collective-permute-start.3 = (f32[2,1,64,128]{3,2,1,0:T(8,128)S(1)}, f32[2,1,64,128]{3,2,1,0:T(8,128)S(1)}, u32[]{:S(2)}, u32[]{:S(2)}) collective-permute-start(f32[2,1,64,128]{3,2,1,0:T(8,128)S(1)} %get-tuple-element.131), channel_id=1, source_target_pairs={{0,1},{1,2},{2,3},{4,5},{5,6},{6,7},{8,9},{9,10},{10,11},{12,13},{... | collective-permute-start | bytes 196616 | tf_op jit(solution)/shard_map/ppermute | solution.py:14
  29.9 1.3 collective-permute-start.2
  31.9 2.4 %collective-permute-done.2 = f32[2,1,64,128]{3,2,1,0:T(8,128)S(1)} collective-permute-done((f32[2,1,64,128]{3,2,1,0:T(8,128)S(1)}, f32[2,1,64,128]{3,2,1,0:T(8,128)S(1)}, u32[]{:S(2)}, u32[]{:S(2)}) %collective-permute-start.2) | collective-permute-done | bytes 65568 | tf_op jit(solution)/shard_map/ppermute | solution.py:17
  34.8 0.5 fusion.19
  35.4 0.6 fusion.77
  38.0 1.4 scatter_fusion.1
  39.4 4.8 %collective-permute-start.5 = (f32[2,1,64,128]{3,2,1,0:T(8,128)S(1)}, f32[2,1,64,128]{3,2,1,0:T(8,128)S(1)}, u32[]{:S(2)}, u32[]{:S(2)}) collective-permute-start(f32[2,1,64,128]{3,2,1,0:T(8,128)S(1)} %get-tuple-element.129), channel_id=1, source_target_pairs={{0,1},{1,2},{2,3},{4,5},{5,6},{6,7},{8,9},{9,10},{10,11},{12,13},{... | collective-permute-start | bytes 196616 | tf_op jit(solution)/shard_map/ppermute | solution.py:14
  44.3 1.3 collective-permute-start.4
  46.1 1.3 collective-permute-done.4
  47.9 0.5 fusion.17
  48.5 0.6 fusion.78
  51.1 1.4 scatter_fusion.2
  52.6 4.3 %collective-permute-start.7 = (f32[2,1,64,128]{3,2,1,0:T(8,128)S(1)}, f32[2,1,64,128]{3,2,1,0:T(8,128)S(1)}, u32[]{:S(2)}, u32[]{:S(2)}) collective-permute-start(f32[2,1,64,128]{3,2,1,0:T(8,128)S(1)} %get-tuple-element.127), channel_id=1, source_target_pairs={{0,1},{1,2},{2,3},{4,5},{5,6},{6,7},{8,9},{9,10},{10,11},{12,13},{... | collective-permute-start | bytes 196616 | tf_op jit(solution)/shard_map/ppermute | solution.py:14
  56.9 1.3 collective-permute-start.6
  58.8 1.3 collective-permute-done.6
  60.5 0.5 fusion.15
  61.2 0.6 fusion.79
  63.8 1.4 scatter_fusion.3
  65.2 4.3 %collective-permute-start.9 = (f32[2,1,64,128]{3,2,1,0:T(8,128)S(1)}, f32[2,1,64,128]{3,2,1,0:T(8,128)S(1)}, u32[]{:S(2)}, u32[]{:S(2)}) collective-permute-start(f32[2,1,64,128]{3,2,1,0:T(8,128)S(1)} %get-tuple-element.125), channel_id=1, source_target_pairs={{0,1},{1,2},{2,3},{4,5},{5,6},{6,7},{8,9},{9,10},{10,11},{12,13},{... | collective-permute-start | bytes 196616 | tf_op jit(solution)/shard_map/ppermute | solution.py:14
  69.5 1.3 collective-permute-start.8
  71.5 1.2 collective-permute-done.8
  73.1 0.5 fusion.13
  73.8 0.7 fusion.80
  76.5 1.4 scatter_fusion.4
  77.9 4.3 %collective-permute-start.11 = (f32[2,1,64,128]{3,2,1,0:T(8,128)S(1)}, f32[2,1,64,128]{3,2,1,0:T(8,128)S(1)}, u32[]{:S(2)}, u32[]{:S(2)}) collective-permute-start(f32[2,1,64,128]{3,2,1,0:T(8,128)S(1)} %get-tuple-element.123), channel_id=1, source_target_pairs={{0,1},{1,2},{2,3},{4,5},{5,6},{6,7},{8,9},{9,10},{10,11},{12,13},{... | collective-permute-start | bytes 196616 | tf_op jit(solution)/shard_map/ppermute | solution.py:14
  82.2 1.5 collective-permute-start.10
  84.4 1.0 collective-permute-done.10
  85.9 0.5 fusion.11
  86.5 0.6 fusion.81
  89.1 1.4 scatter_fusion.5
  90.5 4.3 %collective-permute-start.13 = (f32[2,1,64,128]{3,2,1,0:T(8,128)S(1)}, f32[2,1,64,128]{3,2,1,0:T(8,128)S(1)}, u32[]{:S(2)}, u32[]{:S(2)}) collective-permute-start(f32[2,1,64,128]{3,2,1,0:T(8,128)S(1)} %get-tuple-element.121), channel_id=1, source_target_pairs={{0,1},{1,2},{2,3},{4,5},{5,6},{6,7},{8,9},{9,10},{10,11},{12,13},{... | collective-permute-start | bytes 196616 | tf_op jit(solution)/shard_map/ppermute | solution.py:14
  94.9 1.3 collective-permute-start.12
  96.9 1.2 collective-permute-done.12
  98.5 0.5 fusion.9
  99.2 0.6 fusion.82
  101.8 1.4 scatter_fusion.6
  103.2 4.3 %collective-permute-start.15 = (f32[2,1,64,128]{3,2,1,0:T(8,128)S(1)}, f32[2,1,64,128]{3,2,1,0:T(8,128)S(1)}, u32[]{:S(2)}, u32[]{:S(2)}) collective-permute-start(f32[2,1,64,128]{3,2,1,0:T(8,128)S(1)} %get-tuple-element.119), channel_id=1, source_target_pairs={{0,1},{1,2},{2,3},{4,5},{5,6},{6,7},{8,9},{9,10},{10,11},{12,13},{... | collective-permute-start | bytes 196616 | tf_op jit(solution)/shard_map/ppermute | solution.py:14
  107.5 1.3 collective-permute-start.14
  109.5 1.2 collective-permute-done.14
  111.2 0.5 fusion.7
  111.7 0.5 copy-done.4
  113.0 1.2 fusion.29
  114.2 1.0 fusion.48
  115.3 0.7 fusion.83
  118.0 4.4 %collective-permute-start.17 = (f32[1,1,64,128]{3,2,1,0:T(8,128)S(1)}, f32[1,1,64,128]{3,2,1,0:T(8,128)S(1)}, u32[]{:S(2)}, u32[]{:S(2)}) collective-permute-start(f32[1,1,64,128]{3,2,1,0:T(8,128)S(1)} %get-tuple-element.135), channel_id=1, source_target_pairs={{0,1},{1,2},{2,3},{4,5},{5,6},{6,7},{8,9},{9,10},{10,11},{12,13},{... | collective-permute-start | bytes 98312 | tf_op jit(solution)/shard_map/ppermute | solution.py:14
  122.4 1.3 collective-permute-start.16
  123.7 1.4 scatter_fusion.7
  125.1 27.3 %all-reduce.12.cloned.1.call-done = f32[8,64,128]{2,1,0:T(8,128)} async-done(((f32[8,64,128]{2,1,0:T(8,128)}), f32[8,64,128]{2,1,0:T(8,128)}) %all-reduce.12.cloned.1.call-update) | async-done | bytes 262160 | tf_op jit(solution)/shard_map/psum | solution.py:69
  152.4 1.6 abs_reduce_fusion
  154.3 6.3 %pmax.7 = f32[]{:T(128)} all-reduce(f32[]{:T(128)} %abs_reduce_fusion), channel_id=1, replica_groups=mesh['groups'=2,'shot'=4,'slab'=4] {'slab'}, use_global_device_ids=true, to_apply=%region_10.11 | all-reduce | flops 1 | bytes 8 | tf_op jit(solution)/shard_map/pmax | solution.py:70
  161.3 1.1 fusion.32
  (90 shorter events, 7.1 us)
Async XLA Ops:
  7.2 145.2 %all-reduce.12.cloned.1.call-start = ((), (), s32[]{:S(2)}) async-start(), calls=%async_computation | async-start | bytes 524288 | tf_op jit(solution)/shard_map/psum | solution.py:69
  9.2 9.7 %collective-permute-start.1 = (f32[2,1,64,128]{3,2,1,0:T(8,128)S(1)}, f32[2,1,64,128]{3,2,1,0:T(8,128)S(1)}, u32[]{:S(2)}, u32[]{:S(2)}) collective-permute-start(f32[2,1,64,128]{3,2,1,0:T(8,128)S(1)} %get-tuple-element.133), channel_id=1, source_target_pairs={{0,1},{1,2},{2,3},{4,5},{5,6},{6,7},{8,9},{9,10},{10,11},{12,13},{... | collective-permute-start | bytes 196616 | tf_op jit(solution)/shard_map/ppermute | solution.py:14
  11.6 7.3 %collective-permute-start = (f32[2,1,64,128]{3,2,1,0:T(8,128)S(1)}, f32[2,1,64,128]{3,2,1,0:T(8,128)S(1)}, u32[]{:S(2)}, u32[]{:S(2)}) collective-permute-start(f32[2,1,64,128]{3,2,1,0:T(8,128)S(1)} %get-tuple-element.134), channel_id=1, source_target_pairs={{1,0},{2,1},{3,2},{5,4},{6,5},{7,6},{9,8},{10,9},{11,10},{13,12},{... | collective-permute-start | bytes 196616 | tf_op jit(solution)/shard_map/ppermute | solution.py:17
  19.3 1.0 copy-start
  19.3 1.0 copy-start.1
  19.4 1.1 copy-start.17
  19.4 1.2 copy-start.20
  19.4 1.2 copy-start.21
  20.6 0.8 copy-start.3
  24.8 7.1 %collective-permute-start.3 = (f32[2,1,64,128]{3,2,1,0:T(8,128)S(1)}, f32[2,1,64,128]{3,2,1,0:T(8,128)S(1)}, u32[]{:S(2)}, u32[]{:S(2)}) collective-permute-start(f32[2,1,64,128]{3,2,1,0:T(8,128)S(1)} %get-tuple-element.131), channel_id=1, source_target_pairs={{0,1},{1,2},{2,3},{4,5},{5,6},{6,7},{8,9},{9,10},{10,11},{12,13},{... | collective-permute-start | bytes 196616 | tf_op jit(solution)/shard_map/ppermute | solution.py:14
  29.9 4.4 %collective-permute-start.2 = (f32[2,1,64,128]{3,2,1,0:T(8,128)S(1)}, f32[2,1,64,128]{3,2,1,0:T(8,128)S(1)}, u32[]{:S(2)}, u32[]{:S(2)}) collective-permute-start(f32[2,1,64,128]{3,2,1,0:T(8,128)S(1)} %get-tuple-element.132), channel_id=1, source_target_pairs={{1,0},{2,1},{3,2},{5,4},{6,5},{7,6},{9,8},{10,9},{11,10},{13,12},{... | collective-permute-start | bytes 196616 | tf_op jit(solution)/shard_map/ppermute | solution.py:17
  35.3 0.8 copy-start.5
  39.4 6.7 %collective-permute-start.5 = (f32[2,1,64,128]{3,2,1,0:T(8,128)S(1)}, f32[2,1,64,128]{3,2,1,0:T(8,128)S(1)}, u32[]{:S(2)}, u32[]{:S(2)}) collective-permute-start(f32[2,1,64,128]{3,2,1,0:T(8,128)S(1)} %get-tuple-element.129), channel_id=1, source_target_pairs={{0,1},{1,2},{2,3},{4,5},{5,6},{6,7},{8,9},{9,10},{10,11},{12,13},{... | collective-permute-start | bytes 196616 | tf_op jit(solution)/shard_map/ppermute | solution.py:14
  44.3 3.1 %collective-permute-start.4 = (f32[2,1,64,128]{3,2,1,0:T(8,128)S(1)}, f32[2,1,64,128]{3,2,1,0:T(8,128)S(1)}, u32[]{:S(2)}, u32[]{:S(2)}) collective-permute-start(f32[2,1,64,128]{3,2,1,0:T(8,128)S(1)} %get-tuple-element.130), channel_id=1, source_target_pairs={{1,0},{2,1},{3,2},{5,4},{6,5},{7,6},{9,8},{10,9},{11,10},{13,12},{... | collective-permute-start | bytes 196616 | tf_op jit(solution)/shard_map/ppermute | solution.py:17
  48.4 0.8 copy-start.7
  52.6 6.2 %collective-permute-start.7 = (f32[2,1,64,128]{3,2,1,0:T(8,128)S(1)}, f32[2,1,64,128]{3,2,1,0:T(8,128)S(1)}, u32[]{:S(2)}, u32[]{:S(2)}) collective-permute-start(f32[2,1,64,128]{3,2,1,0:T(8,128)S(1)} %get-tuple-element.127), channel_id=1, source_target_pairs={{0,1},{1,2},{2,3},{4,5},{5,6},{6,7},{8,9},{9,10},{10,11},{12,13},{... | collective-permute-start | bytes 196616 | tf_op jit(solution)/shard_map/ppermute | solution.py:14
  56.9 3.1 %collective-permute-start.6 = (f32[2,1,64,128]{3,2,1,0:T(8,128)S(1)}, f32[2,1,64,128]{3,2,1,0:T(8,128)S(1)}, u32[]{:S(2)}, u32[]{:S(2)}) collective-permute-start(f32[2,1,64,128]{3,2,1,0:T(8,128)S(1)} %get-tuple-element.128), channel_id=1, source_target_pairs={{1,0},{2,1},{3,2},{5,4},{6,5},{7,6},{9,8},{10,9},{11,10},{13,12},{... | collective-permute-start | bytes 196616 | tf_op jit(solution)/shard_map/ppermute | solution.py:17
  61.0 0.8 copy-start.9
  65.2 6.3 %collective-permute-start.9 = (f32[2,1,64,128]{3,2,1,0:T(8,128)S(1)}, f32[2,1,64,128]{3,2,1,0:T(8,128)S(1)}, u32[]{:S(2)}, u32[]{:S(2)}) collective-permute-start(f32[2,1,64,128]{3,2,1,0:T(8,128)S(1)} %get-tuple-element.125), channel_id=1, source_target_pairs={{0,1},{1,2},{2,3},{4,5},{5,6},{6,7},{8,9},{9,10},{10,11},{12,13},{... | collective-permute-start | bytes 196616 | tf_op jit(solution)/shard_map/ppermute | solution.py:14
  69.5 3.1 %collective-permute-start.8 = (f32[2,1,64,128]{3,2,1,0:T(8,128)S(1)}, f32[2,1,64,128]{3,2,1,0:T(8,128)S(1)}, u32[]{:S(2)}, u32[]{:S(2)}) collective-permute-start(f32[2,1,64,128]{3,2,1,0:T(8,128)S(1)} %get-tuple-element.126), channel_id=1, source_target_pairs={{1,0},{2,1},{3,2},{5,4},{6,5},{7,6},{9,8},{10,9},{11,10},{13,12},{... | collective-permute-start | bytes 196616 | tf_op jit(solution)/shard_map/ppermute | solution.py:17
  73.6 0.8 copy-start.11
  77.9 6.5 %collective-permute-start.11 = (f32[2,1,64,128]{3,2,1,0:T(8,128)S(1)}, f32[2,1,64,128]{3,2,1,0:T(8,128)S(1)}, u32[]{:S(2)}, u32[]{:S(2)}) collective-permute-start(f32[2,1,64,128]{3,2,1,0:T(8,128)S(1)} %get-tuple-element.123), channel_id=1, source_target_pairs={{0,1},{1,2},{2,3},{4,5},{5,6},{6,7},{8,9},{9,10},{10,11},{12,13},{... | collective-permute-start | bytes 196616 | tf_op jit(solution)/shard_map/ppermute | solution.py:14
  82.2 3.1 %collective-permute-start.10 = (f32[2,1,64,128]{3,2,1,0:T(8,128)S(1)}, f32[2,1,64,128]{3,2,1,0:T(8,128)S(1)}, u32[]{:S(2)}, u32[]{:S(2)}) collective-permute-start(f32[2,1,64,128]{3,2,1,0:T(8,128)S(1)} %get-tuple-element.124), channel_id=1, source_target_pairs={{1,0},{2,1},{3,2},{5,4},{6,5},{7,6},{9,8},{10,9},{11,10},{13,12},{... | collective-permute-start | bytes 196616 | tf_op jit(solution)/shard_map/ppermute | solution.py:17
  86.4 0.8 copy-start.13
  90.5 6.3 %collective-permute-start.13 = (f32[2,1,64,128]{3,2,1,0:T(8,128)S(1)}, f32[2,1,64,128]{3,2,1,0:T(8,128)S(1)}, u32[]{:S(2)}, u32[]{:S(2)}) collective-permute-start(f32[2,1,64,128]{3,2,1,0:T(8,128)S(1)} %get-tuple-element.121), channel_id=1, source_target_pairs={{0,1},{1,2},{2,3},{4,5},{5,6},{6,7},{8,9},{9,10},{10,11},{12,13},{... | collective-permute-start | bytes 196616 | tf_op jit(solution)/shard_map/ppermute | solution.py:14
  94.9 3.1 %collective-permute-start.12 = (f32[2,1,64,128]{3,2,1,0:T(8,128)S(1)}, f32[2,1,64,128]{3,2,1,0:T(8,128)S(1)}, u32[]{:S(2)}, u32[]{:S(2)}) collective-permute-start(f32[2,1,64,128]{3,2,1,0:T(8,128)S(1)} %get-tuple-element.122), channel_id=1, source_target_pairs={{1,0},{2,1},{3,2},{5,4},{6,5},{7,6},{9,8},{10,9},{11,10},{13,12},{... | collective-permute-start | bytes 196616 | tf_op jit(solution)/shard_map/ppermute | solution.py:17
  99.0 0.8 copy-start.15
  103.2 6.3 %collective-permute-start.15 = (f32[2,1,64,128]{3,2,1,0:T(8,128)S(1)}, f32[2,1,64,128]{3,2,1,0:T(8,128)S(1)}, u32[]{:S(2)}, u32[]{:S(2)}) collective-permute-start(f32[2,1,64,128]{3,2,1,0:T(8,128)S(1)} %get-tuple-element.119), channel_id=1, source_target_pairs={{0,1},{1,2},{2,3},{4,5},{5,6},{6,7},{8,9},{9,10},{10,11},{12,13},{... | collective-permute-start | bytes 196616 | tf_op jit(solution)/shard_map/ppermute | solution.py:14
  107.5 3.1 %collective-permute-start.14 = (f32[2,1,64,128]{3,2,1,0:T(8,128)S(1)}, f32[2,1,64,128]{3,2,1,0:T(8,128)S(1)}, u32[]{:S(2)}, u32[]{:S(2)}) collective-permute-start(f32[2,1,64,128]{3,2,1,0:T(8,128)S(1)} %get-tuple-element.120), channel_id=1, source_target_pairs={{1,0},{2,1},{3,2},{5,4},{6,5},{7,6},{9,8},{10,9},{11,10},{13,12},{... | collective-permute-start | bytes 196616 | tf_op jit(solution)/shard_map/ppermute | solution.py:17
  110.7 1.0 copy-start.16
  111.2 1.1 copy-start.4
  111.2 1.2 copy-start.6
  111.2 1.4 copy-start.8
  111.2 1.5 copy-start.10
  111.2 1.7 copy-start.12
  111.2 1.8 %copy-start.14 = (f32[2,8,64,128]{3,2,1,0:T(8,128)S(1)}, f32[2,8,64,128]{3,2,1,0:T(8,128)}, u32[]{:S(2)}) copy-start(f32[2,8,64,128]{3,2,1,0:T(8,128)} %copy-done.13) | copy-start | bytes 1572868
  113.0 1.2 copy-start.2
  118.0 36.0 %collective-permute-start.17 = (f32[1,1,64,128]{3,2,1,0:T(8,128)S(1)}, f32[1,1,64,128]{3,2,1,0:T(8,128)S(1)}, u32[]{:S(2)}, u32[]{:S(2)}) collective-permute-start(f32[1,1,64,128]{3,2,1,0:T(8,128)S(1)} %get-tuple-element.135), channel_id=1, source_target_pairs={{0,1},{1,2},{2,3},{4,5},{5,6},{6,7},{8,9},{9,10},{10,11},{12,13},{... | collective-permute-start | bytes 98312 | tf_op jit(solution)/shard_map/ppermute | solution.py:14
  122.4 31.6 %collective-permute-start.16 = (f32[1,1,64,128]{3,2,1,0:T(8,128)S(1)}, f32[1,1,64,128]{3,2,1,0:T(8,128)S(1)}, u32[]{:S(2)}, u32[]{:S(2)}) collective-permute-start(f32[1,1,64,128]{3,2,1,0:T(8,128)S(1)} %get-tuple-element.136), channel_id=1, source_target_pairs={{1,0},{2,1},{3,2},{5,4},{6,5},{7,6},{9,8},{10,9},{11,10},{13,12},{... | collective-permute-start | bytes 98312 | tf_op jit(solution)/shard_map/ppermute | solution.py:17
  125.1 37.2 %copy-start.18 = (f32[65536]{0:T(1024)}, f32[65536]{0:T(1024)S(1)}, u32[]{:S(2)}) copy-start(f32[65536]{0:T(1024)S(1)} %scatter_fusion.7) | copy-start | bytes 786436
  152.4 8.9 %copy-start.19 = (f32[8,64,128]{2,1,0:T(8,128)S(1)}, f32[8,64,128]{2,1,0:T(8,128)}, u32[]{:S(2)}) copy-start(f32[8,64,128]{2,1,0:T(8,128)} %all-reduce.12.cloned.1.call-done) | copy-start | bytes 786436
Sparse Core Ops, SparseCore 0:
  114.4 37.9 all-reduce.11
where the time goes:
time: 170 us; the launch traced here: 169 us
  starting transfers between devices  50.2 us (30%)
  waiting for transfers between devices  36.8 us (22%)
  between operations  36 us (21%)
  other arithmetic  33.2 us (20%)
  local copies, waits for them, and re-layouts  6.66 us (4%)
  blocking collectives  6.3 us (4%)
    ppermute x9, starting transfers between devices, extended(): lax.ppermute(lax.slice_in_dim(block, block.shape[dim] - width, None, axis...  38.4 us
    psum x1, waiting for transfers between devices, per_device(): gradient = lax.psum(local_image, 'shot')  27.3 us
    ppermute x9, starting transfers between devices, extended(): lax.ppermute(lax.slice_in_dim(block, 0, width, axis=dim), axis, backward)  11.8 us
    scatter-add x8, other arithmetic, inject(): flat = flat.at[rows, local].add(jnp.where(valid, values, 0.0))  11.2 us
    ppermute x9, waiting for transfers between devices, extended(): lax.ppermute(lax.slice_in_dim(block, 0, width, axis=dim), axis, backward)  9.49 us
    pmax x1, blocking collectives, per_device(): peak = lax.pmax(jnp.max(jnp.abs(gradient)), 'slab')  6.3 us
    add x8, other arithmetic, inject(): flat = flat.at[rows, local].add(jnp.where(valid, values, 0.0))  5.13 us
    sub x8, other arithmetic, local_laplace(): return beside - 6.0 * center  4.02 us
  transfers between devices with their start and end apart: 19, of which 8 were waited for; matrix products, arithmetic and copies ran while one was open for 6% of the time, Pallas kernels for 0%

commit v1 on v0

--- a/solution.py
+++ b/solution.py
@@ -66,7 +66,7 @@
         wave_later, wave = (wave, wave_prior)
         adjoint_later, adjoint = (adjoint, adjoint_prior)
     local_image = jnp.sum(image, axis=0)
-    gradient = lax.psum(local_image, "shot")
+    gradient = jnp.sum(lax.all_gather(local_image, "shot"), axis=0)
     peak = lax.pmax(jnp.max(jnp.abs(gradient)), "slab")
     new_model = update(model, gradient, peak)
     padded_wave = extended(wave, (("slab", 1),), 1)

time: 170 us -> 164 us (0.965)
  waiting for transfers between devices: 36.8 us -> 29.5 us
    psum x1 -> x0, waiting for transfers between devices: 27.3 us -> none  [per_device(): gradient = lax.psum(local_image, 'shot')]
    all_gather x0 -> x1, waiting for transfers between devices: none -> 19.2 us  [per_device(): gradient = jnp.sum(lax.all_gather(local_image, 'shot'), axis=0)]
where the time goes in v1:
time: 164 us; the launch traced here: 163 us
  starting transfers between devices  50.2 us (31%)
  between operations  36.2 us (22%)
  other arithmetic  33.6 us (20%)
  waiting for transfers between devices  29.5 us (18%)
  blocking collectives  6.72 us (4%)
  local copies, waits for them, and re-layouts  6.63 us (4%)
    ppermute x9, starting transfers between devices, extended(): lax.ppermute(lax.slice_in_dim(block, block.shape[dim] - width, None, axis...  38.4 us
    all_gather x1, waiting for transfers between devices, per_device(): gradient = jnp.sum(lax.all_gather(local_image, 'shot'), axis=0)  19.2 us
    ppermute x9, starting transfers between devices, extended(): lax.ppermute(lax.slice_in_dim(block, 0, width, axis=dim), axis, backward)  11.8 us
    scatter-add x8, other arithmetic, inject(): flat = flat.at[rows, local].add(jnp.where(valid, values, 0.0))  11.2 us
    ppermute x9, waiting for transfers between devices, extended(): lax.ppermute(lax.slice_in_dim(block, 0, width, axis=dim), axis, backward)  10.2 us
    pmax x1, blocking collectives, per_device(): peak = lax.pmax(jnp.max(jnp.abs(gradient)), 'slab')  6.72 us
    add x8, other arithmetic, inject(): flat = flat.at[rows, local].add(jnp.where(valid, values, 0.0))  5.27 us
    sub x8, other arithmetic, local_laplace(): return beside - 6.0 * center  4.02 us
  transfers between devices with their start and end apart: 19, of which 8 were waited for; matrix products, arithmetic and copies ran while one was open for 6% of the time, Pallas kernels for 0%

profile of v1, /device:TPU:0, one launch (start us, length us, event | category | flops | bytes accessed | tf_op | source)
XLA Modules:
  0.0 162.8 jit_solution(2310037785842486905)
XLA Ops:
  7.2 1.0 constant_dynamic-update-slice_fusion.1
  8.2 1.0 constant_dynamic-update-slice_fusion
  9.2 2.4 %collective-permute-start.1 = (f32[2,1,64,128]{3,2,1,0:T(8,128)S(1)}, f32[2,1,64,128]{3,2,1,0:T(8,128)S(1)}, u32[]{:S(2)}, u32[]{:S(2)}) collective-permute-start(f32[2,1,64,128]{3,2,1,0:T(8,128)S(1)} %get-tuple-element.133), channel_id=1, source_target_pairs={{0,1},{1,2},{2,3},{4,5},{5,6},{6,7},{8,9},{9,10},{10,11},{12,13},{... | collective-permute-start | bytes 196616 | tf_op jit(solution)/shard_map/ppermute | solution.py:14
  11.6 1.3 collective-permute-start
  13.5 0.7 fusion.64
  14.2 0.7 fusion.65
  14.9 0.9 fusion.66
  15.9 1.6 %fusion.75 = (f32[1,1]{1,0:T(1,128)}, f32[1,1]{1,0:T(1,128)}, f32[1,1]{1,0:T(1,128)}, f32[1,1]{1,0:T(1,128)}, f32[1,1]{1,0:T(1,128)}, /*index=5*/f32[1,1]{1,0:T(1,128)}, f32[1,1]{1,0:T(1,128)}, f32[1,1]{1,0:T(1,128)}) fusion(f32[1,8]{1,0:T(1,128)} %param.30), kind=kLoop, calls=%fused_computation.261 | loop fusion | bytes 64 | tf_op jit(solution)/shard_map/slice | solution.py:63
  18.2 0.7 and_reduce_fusion
  19.4 0.5 fusion.27
  20.8 0.7 fusion.76
  23.5 1.4 scatter_fusion
  24.9 5.1 %collective-permute-start.3 = (f32[2,1,64,128]{3,2,1,0:T(8,128)S(1)}, f32[2,1,64,128]{3,2,1,0:T(8,128)S(1)}, u32[]{:S(2)}, u32[]{:S(2)}) collective-permute-start(f32[2,1,64,128]{3,2,1,0:T(8,128)S(1)} %get-tuple-element.131), channel_id=1, source_target_pairs={{0,1},{1,2},{2,3},{4,5},{5,6},{6,7},{8,9},{9,10},{10,11},{12,13},{... | collective-permute-start | bytes 196616 | tf_op jit(solution)/shard_map/ppermute | solution.py:14
  30.0 1.3 collective-permute-start.2
  31.9 2.5 %collective-permute-done.2 = f32[2,1,64,128]{3,2,1,0:T(8,128)S(1)} collective-permute-done((f32[2,1,64,128]{3,2,1,0:T(8,128)S(1)}, f32[2,1,64,128]{3,2,1,0:T(8,128)S(1)}, u32[]{:S(2)}, u32[]{:S(2)}) %collective-permute-start.2) | collective-permute-done | bytes 65568 | tf_op jit(solution)/shard_map/ppermute | solution.py:17
  34.8 0.5 fusion.19
  35.5 0.7 fusion.77
  38.2 1.4 scatter_fusion.1
  39.7 4.8 %collective-permute-start.5 = (f32[2,1,64,128]{3,2,1,0:T(8,128)S(1)}, f32[2,1,64,128]{3,2,1,0:T(8,128)S(1)}, u32[]{:S(2)}, u32[]{:S(2)}) collective-permute-start(f32[2,1,64,128]{3,2,1,0:T(8,128)S(1)} %get-tuple-element.129), channel_id=1, source_target_pairs={{0,1},{1,2},{2,3},{4,5},{5,6},{6,7},{8,9},{9,10},{10,11},{12,13},{... | collective-permute-start | bytes 196616 | tf_op jit(solution)/shard_map/ppermute | solution.py:14
  44.5 1.3 collective-permute-start.4
  46.4 1.3 collective-permute-done.4
  48.1 0.5 fusion.17
  48.8 0.6 fusion.78
  51.3 1.4 scatter_fusion.2
  52.8 4.3 %collective-permute-start.7 = (f32[2,1,64,128]{3,2,1,0:T(8,128)S(1)}, f32[2,1,64,128]{3,2,1,0:T(8,128)S(1)}, u32[]{:S(2)}, u32[]{:S(2)}) collective-permute-start(f32[2,1,64,128]{3,2,1,0:T(8,128)S(1)} %get-tuple-element.127), channel_id=1, source_target_pairs={{0,1},{1,2},{2,3},{4,5},{5,6},{6,7},{8,9},{9,10},{10,11},{12,13},{... | collective-permute-start | bytes 196616 | tf_op jit(solution)/shard_map/ppermute | solution.py:14
  57.1 1.3 collective-permute-start.6
  59.0 1.3 collective-permute-done.6
  60.7 0.5 fusion.15
  61.4 0.6 fusion.79
  64.0 1.4 scatter_fusion.3
  65.4 4.3 %collective-permute-start.9 = (f32[2,1,64,128]{3,2,1,0:T(8,128)S(1)}, f32[2,1,64,128]{3,2,1,0:T(8,128)S(1)}, u32[]{:S(2)}, u32[]{:S(2)}) collective-permute-start(f32[2,1,64,128]{3,2,1,0:T(8,128)S(1)} %get-tuple-element.125), channel_id=1, source_target_pairs={{0,1},{1,2},{2,3},{4,5},{5,6},{6,7},{8,9},{9,10},{10,11},{12,13},{... | collective-permute-start | bytes 196616 | tf_op jit(solution)/shard_map/ppermute | solution.py:14
  69.7 1.3 collective-permute-start.8
  71.7 1.2 collective-permute-done.8
  73.3 0.5 fusion.13
  74.0 0.7 fusion.80
  76.7 1.4 scatter_fusion.4
  78.1 4.3 %collective-permute-start.11 = (f32[2,1,64,128]{3,2,1,0:T(8,128)S(1)}, f32[2,1,64,128]{3,2,1,0:T(8,128)S(1)}, u32[]{:S(2)}, u32[]{:S(2)}) collective-permute-start(f32[2,1,64,128]{3,2,1,0:T(8,128)S(1)} %get-tuple-element.123), channel_id=1, source_target_pairs={{0,1},{1,2},{2,3},{4,5},{5,6},{6,7},{8,9},{9,10},{10,11},{12,13},{... | collective-permute-start | bytes 196616 | tf_op jit(solution)/shard_map/ppermute | solution.py:14
  82.5 1.5 collective-permute-start.10
  84.6 1.0 collective-permute-done.10
  86.1 0.5 fusion.11
  86.7 0.7 fusion.81
  89.5 1.4 scatter_fusion.5
  90.9 4.3 %collective-permute-start.13 = (f32[2,1,64,128]{3,2,1,0:T(8,128)S(1)}, f32[2,1,64,128]{3,2,1,0:T(8,128)S(1)}, u32[]{:S(2)}, u32[]{:S(2)}) collective-permute-start(f32[2,1,64,128]{3,2,1,0:T(8,128)S(1)} %get-tuple-element.121), channel_id=1, source_target_pairs={{0,1},{1,2},{2,3},{4,5},{5,6},{6,7},{8,9},{9,10},{10,11},{12,13},{... | collective-permute-start | bytes 196616 | tf_op jit(solution)/shard_map/ppermute | solution.py:14
  95.3 1.3 collective-permute-start.12
  97.2 1.2 collective-permute-done.12
  98.9 0.5 fusion.9
  99.5 0.7 fusion.82
  102.3 1.4 scatter_fusion.6
  103.7 4.3 %collective-permute-start.15 = (f32[2,1,64,128]{3,2,1,0:T(8,128)S(1)}, f32[2,1,64,128]{3,2,1,0:T(8,128)S(1)}, u32[]{:S(2)}, u32[]{:S(2)}) collective-permute-start(f32[2,1,64,128]{3,2,1,0:T(8,128)S(1)} %get-tuple-element.119), channel_id=1, source_target_pairs={{0,1},{1,2},{2,3},{4,5},{5,6},{6,7},{8,9},{9,10},{10,11},{12,13},{... | collective-permute-start | bytes 196616 | tf_op jit(solution)/shard_map/ppermute | solution.py:14
  108.1 1.3 collective-permute-start.14
  109.4 1.8 %collective-permute-done.14 = f32[2,1,64,128]{3,2,1,0:T(8,128)S(1)} collective-permute-done((f32[2,1,64,128]{3,2,1,0:T(8,128)S(1)}, f32[2,1,64,128]{3,2,1,0:T(8,128)S(1)}, u32[]{:S(2)}, u32[]{:S(2)}) %collective-permute-start.14) | collective-permute-done | bytes 65568 | tf_op jit(solution)/shard_map/ppermute | solution.py:17
  111.7 0.5 fusion.7
  112.3 0.5 copy-done.4
  113.5 1.2 fusion.29
  115.3 1.0 fusion.48
  116.3 0.7 fusion.83
  119.0 4.4 %collective-permute-start.17 = (f32[1,1,64,128]{3,2,1,0:T(8,128)S(1)}, f32[1,1,64,128]{3,2,1,0:T(8,128)S(1)}, u32[]{:S(2)}, u32[]{:S(2)}) collective-permute-start(f32[1,1,64,128]{3,2,1,0:T(8,128)S(1)} %get-tuple-element.135), channel_id=1, source_target_pairs={{0,1},{1,2},{2,3},{4,5},{5,6},{6,7},{8,9},{9,10},{10,11},{12,13},{... | collective-permute-start | bytes 98312 | tf_op jit(solution)/shard_map/ppermute | solution.py:14
  123.4 1.3 collective-permute-start.16
  124.7 1.4 scatter_fusion.7
  126.1 19.2 %all-gather.2.cloned.1.call-done = f32[4,8,64,128]{3,2,1,0:T(8,128)} async-done(((f32[1,8,64,128]{3,2,1,0:T(8,128)}), f32[4,8,64,128]{3,2,1,0:T(8,128)}) %all-gather.2.cloned.1.call-update) | async-done | bytes 1048592 | tf_op jit(solution)/shard_map/all_gather | solution.py:69
  145.3 1.3 reduce_sum.8
  146.6 0.6 abs_reduce_fusion
  147.5 6.7 %pmax.7 = f32[]{:T(128)} all-reduce(f32[]{:T(128)} %abs_reduce_fusion), channel_id=1, replica_groups=mesh['groups'=2,'shot'=4,'slab'=4] {'slab'}, use_global_device_ids=true, to_apply=%region_10.11 | all-reduce | flops 1 | bytes 8 | tf_op jit(solution)/shard_map/pmax | solution.py:70
  154.9 1.1 fusion.32
  (89 shorter events, 7.5 us)
Async XLA Ops:
  7.2 138.1 %all-gather.2.cloned.1.call-start = ((), (), s32[]{:S(2)}) async-start(), calls=%async_computation | async-start | bytes 1310720 | tf_op jit(solution)/shard_map/all_gather | solution.py:69
  9.2 9.7 %collective-permute-start.1 = (f32[2,1,64,128]{3,2,1,0:T(8,128)S(1)}, f32[2,1,64,128]{3,2,1,0:T(8,128)S(1)}, u32[]{:S(2)}, u32[]{:S(2)}) collective-permute-start(f32[2,1,64,128]{3,2,1,0:T(8,128)S(1)} %get-tuple-element.133), channel_id=1, source_target_pairs={{0,1},{1,2},{2,3},{4,5},{5,6},{6,7},{8,9},{9,10},{10,11},{12,13},{... | collective-permute-start | bytes 196616 | tf_op jit(solution)/shard_map/ppermute | solution.py:14
  11.6 7.3 %collective-permute-start = (f32[2,1,64,128]{3,2,1,0:T(8,128)S(1)}, f32[2,1,64,128]{3,2,1,0:T(8,128)S(1)}, u32[]{:S(2)}, u32[]{:S(2)}) collective-permute-start(f32[2,1,64,128]{3,2,1,0:T(8,128)S(1)} %get-tuple-element.134), channel_id=1, source_target_pairs={{1,0},{2,1},{3,2},{5,4},{6,5},{7,6},{9,8},{10,9},{11,10},{13,12},{... | collective-permute-start | bytes 196616 | tf_op jit(solution)/shard_map/ppermute | solution.py:17
  19.3 1.0 copy-start
  19.3 1.0 copy-start.1
  19.4 1.1 copy-start.17
  19.4 1.2 copy-start.19
  19.4 1.2 copy-start.20
  20.6 0.8 copy-start.3
  24.9 7.0 %collective-permute-start.3 = (f32[2,1,64,128]{3,2,1,0:T(8,128)S(1)}, f32[2,1,64,128]{3,2,1,0:T(8,128)S(1)}, u32[]{:S(2)}, u32[]{:S(2)}) collective-permute-start(f32[2,1,64,128]{3,2,1,0:T(8,128)S(1)} %get-tuple-element.131), channel_id=1, source_target_pairs={{0,1},{1,2},{2,3},{4,5},{5,6},{6,7},{8,9},{9,10},{10,11},{12,13},{... | collective-permute-start | bytes 196616 | tf_op jit(solution)/shard_map/ppermute | solution.py:14
  30.0 4.4 %collective-permute-start.2 = (f32[2,1,64,128]{3,2,1,0:T(8,128)S(1)}, f32[2,1,64,128]{3,2,1,0:T(8,128)S(1)}, u32[]{:S(2)}, u32[]{:S(2)}) collective-permute-start(f32[2,1,64,128]{3,2,1,0:T(8,128)S(1)} %get-tuple-element.132), channel_id=1, source_target_pairs={{1,0},{2,1},{3,2},{5,4},{6,5},{7,6},{9,8},{10,9},{11,10},{13,12},{... | collective-permute-start | bytes 196616 | tf_op jit(solution)/shard_map/ppermute | solution.py:17
  35.3 0.8 copy-start.5
  39.7 6.7 %collective-permute-start.5 = (f32[2,1,64,128]{3,2,1,0:T(8,128)S(1)}, f32[2,1,64,128]{3,2,1,0:T(8,128)S(1)}, u32[]{:S(2)}, u32[]{:S(2)}) collective-permute-start(f32[2,1,64,128]{3,2,1,0:T(8,128)S(1)} %get-tuple-element.129), channel_id=1, source_target_pairs={{0,1},{1,2},{2,3},{4,5},{5,6},{6,7},{8,9},{9,10},{10,11},{12,13},{... | collective-permute-start | bytes 196616 | tf_op jit(solution)/shard_map/ppermute | solution.py:14
  44.5 3.1 %collective-permute-start.4 = (f32[2,1,64,128]{3,2,1,0:T(8,128)S(1)}, f32[2,1,64,128]{3,2,1,0:T(8,128)S(1)}, u32[]{:S(2)}, u32[]{:S(2)}) collective-permute-start(f32[2,1,64,128]{3,2,1,0:T(8,128)S(1)} %get-tuple-element.130), channel_id=1, source_target_pairs={{1,0},{2,1},{3,2},{5,4},{6,5},{7,6},{9,8},{10,9},{11,10},{13,12},{... | collective-permute-start | bytes 196616 | tf_op jit(solution)/shard_map/ppermute | solution.py:17
  48.6 0.8 copy-start.7
  52.8 6.2 %collective-permute-start.7 = (f32[2,1,64,128]{3,2,1,0:T(8,128)S(1)}, f32[2,1,64,128]{3,2,1,0:T(8,128)S(1)}, u32[]{:S(2)}, u32[]{:S(2)}) collective-permute-start(f32[2,1,64,128]{3,2,1,0:T(8,128)S(1)} %get-tuple-element.127), channel_id=1, source_target_pairs={{0,1},{1,2},{2,3},{4,5},{5,6},{6,7},{8,9},{9,10},{10,11},{12,13},{... | collective-permute-start | bytes 196616 | tf_op jit(solution)/shard_map/ppermute | solution.py:14
  57.1 3.1 %collective-permute-start.6 = (f32[2,1,64,128]{3,2,1,0:T(8,128)S(1)}, f32[2,1,64,128]{3,2,1,0:T(8,128)S(1)}, u32[]{:S(2)}, u32[]{:S(2)}) collective-permute-start(f32[2,1,64,128]{3,2,1,0:T(8,128)S(1)} %get-tuple-element.128), channel_id=1, source_target_pairs={{1,0},{2,1},{3,2},{5,4},{6,5},{7,6},{9,8},{10,9},{11,10},{13,12},{... | collective-permute-start | bytes 196616 | tf_op jit(solution)/shard_map/ppermute | solution.py:17
  61.2 0.8 copy-start.9
  65.4 6.3 %collective-permute-start.9 = (f32[2,1,64,128]{3,2,1,0:T(8,128)S(1)}, f32[2,1,64,128]{3,2,1,0:T(8,128)S(1)}, u32[]{:S(2)}, u32[]{:S(2)}) collective-permute-start(f32[2,1,64,128]{3,2,1,0:T(8,128)S(1)} %get-tuple-element.125), channel_id=1, source_target_pairs={{0,1},{1,2},{2,3},{4,5},{5,6},{6,7},{8,9},{9,10},{10,11},{12,13},{... | collective-permute-start | bytes 196616 | tf_op jit(solution)/shard_map/ppermute | solution.py:14
  69.7 3.1 %collective-permute-start.8 = (f32[2,1,64,128]{3,2,1,0:T(8,128)S(1)}, f32[2,1,64,128]{3,2,1,0:T(8,128)S(1)}, u32[]{:S(2)}, u32[]{:S(2)}) collective-permute-start(f32[2,1,64,128]{3,2,1,0:T(8,128)S(1)} %get-tuple-element.126), channel_id=1, source_target_pairs={{1,0},{2,1},{3,2},{5,4},{6,5},{7,6},{9,8},{10,9},{11,10},{13,12},{... | collective-permute-start | bytes 196616 | tf_op jit(solution)/shard_map/ppermute | solution.py:17
  73.8 0.8 copy-start.11
  78.1 6.5 %collective-permute-start.11 = (f32[2,1,64,128]{3,2,1,0:T(8,128)S(1)}, f32[2,1,64,128]{3,2,1,0:T(8,128)S(1)}, u32[]{:S(2)}, u32[]{:S(2)}) collective-permute-start(f32[2,1,64,128]{3,2,1,0:T(8,128)S(1)} %get-tuple-element.123), channel_id=1, source_target_pairs={{0,1},{1,2},{2,3},{4,5},{5,6},{6,7},{8,9},{9,10},{10,11},{12,13},{... | collective-permute-start | bytes 196616 | tf_op jit(solution)/shard_map/ppermute | solution.py:14
  82.5 3.1 %collective-permute-start.10 = (f32[2,1,64,128]{3,2,1,0:T(8,128)S(1)}, f32[2,1,64,128]{3,2,1,0:T(8,128)S(1)}, u32[]{:S(2)}, u32[]{:S(2)}) collective-permute-start(f32[2,1,64,128]{3,2,1,0:T(8,128)S(1)} %get-tuple-element.124), channel_id=1, source_target_pairs={{1,0},{2,1},{3,2},{5,4},{6,5},{7,6},{9,8},{10,9},{11,10},{13,12},{... | collective-permute-start | bytes 196616 | tf_op jit(solution)/shard_map/ppermute | solution.py:17
  86.6 0.8 copy-start.13
  90.9 6.3 %collective-permute-start.13 = (f32[2,1,64,128]{3,2,1,0:T(8,128)S(1)}, f32[2,1,64,128]{3,2,1,0:T(8,128)S(1)}, u32[]{:S(2)}, u32[]{:S(2)}) collective-permute-start(f32[2,1,64,128]{3,2,1,0:T(8,128)S(1)} %get-tuple-element.121), channel_id=1, source_target_pairs={{0,1},{1,2},{2,3},{4,5},{5,6},{6,7},{8,9},{9,10},{10,11},{12,13},{... | collective-permute-start | bytes 196616 | tf_op jit(solution)/shard_map/ppermute | solution.py:14
  95.3 3.1 %collective-permute-start.12 = (f32[2,1,64,128]{3,2,1,0:T(8,128)S(1)}, f32[2,1,64,128]{3,2,1,0:T(8,128)S(1)}, u32[]{:S(2)}, u32[]{:S(2)}) collective-permute-start(f32[2,1,64,128]{3,2,1,0:T(8,128)S(1)} %get-tuple-element.122), channel_id=1, source_target_pairs={{1,0},{2,1},{3,2},{5,4},{6,5},{7,6},{9,8},{10,9},{11,10},{13,12},{... | collective-permute-start | bytes 196616 | tf_op jit(solution)/shard_map/ppermute | solution.py:17
  99.4 0.8 copy-start.15
  103.7 5.6 %collective-permute-start.15 = (f32[2,1,64,128]{3,2,1,0:T(8,128)S(1)}, f32[2,1,64,128]{3,2,1,0:T(8,128)S(1)}, u32[]{:S(2)}, u32[]{:S(2)}) collective-permute-start(f32[2,1,64,128]{3,2,1,0:T(8,128)S(1)} %get-tuple-element.119), channel_id=1, source_target_pairs={{0,1},{1,2},{2,3},{4,5},{5,6},{6,7},{8,9},{9,10},{10,11},{12,13},{... | collective-permute-start | bytes 196616 | tf_op jit(solution)/shard_map/ppermute | solution.py:14
  108.1 3.1 %collective-permute-start.14 = (f32[2,1,64,128]{3,2,1,0:T(8,128)S(1)}, f32[2,1,64,128]{3,2,1,0:T(8,128)S(1)}, u32[]{:S(2)}, u32[]{:S(2)}) collective-permute-start(f32[2,1,64,128]{3,2,1,0:T(8,128)S(1)} %get-tuple-element.120), channel_id=1, source_target_pairs={{1,0},{2,1},{3,2},{5,4},{6,5},{7,6},{9,8},{10,9},{11,10},{13,12},{... | collective-permute-start | bytes 196616 | tf_op jit(solution)/shard_map/ppermute | solution.py:17
  111.2 1.0 copy-start.16
  111.7 1.1 copy-start.4
  111.7 1.2 copy-start.6
  111.7 1.4 copy-start.8
  111.7 1.5 copy-start.10
  111.7 1.7 %copy-start.12 = (f32[2,8,64,128]{3,2,1,0:T(8,128)S(1)}, f32[2,8,64,128]{3,2,1,0:T(8,128)}, u32[]{:S(2)}) copy-start(f32[2,8,64,128]{3,2,1,0:T(8,128)} %copy-done.11) | copy-start | bytes 1572868
  111.7 1.8 %copy-start.14 = (f32[2,8,64,128]{3,2,1,0:T(8,128)S(1)}, f32[2,8,64,128]{3,2,1,0:T(8,128)}, u32[]{:S(2)}) copy-start(f32[2,8,64,128]{3,2,1,0:T(8,128)} %copy-done.13) | copy-start | bytes 1572868
  113.5 1.2 copy-start.2
  119.0 28.2 %collective-permute-start.17 = (f32[1,1,64,128]{3,2,1,0:T(8,128)S(1)}, f32[1,1,64,128]{3,2,1,0:T(8,128)S(1)}, u32[]{:S(2)}, u32[]{:S(2)}) collective-permute-start(f32[1,1,64,128]{3,2,1,0:T(8,128)S(1)} %get-tuple-element.135), channel_id=1, source_target_pairs={{0,1},{1,2},{2,3},{4,5},{5,6},{6,7},{8,9},{9,10},{10,11},{12,13},{... | collective-permute-start | bytes 98312 | tf_op jit(solution)/shard_map/ppermute | solution.py:14
  123.4 23.8 %collective-permute-start.16 = (f32[1,1,64,128]{3,2,1,0:T(8,128)S(1)}, f32[1,1,64,128]{3,2,1,0:T(8,128)S(1)}, u32[]{:S(2)}, u32[]{:S(2)}) collective-permute-start(f32[1,1,64,128]{3,2,1,0:T(8,128)S(1)} %get-tuple-element.136), channel_id=1, source_target_pairs={{1,0},{2,1},{3,2},{5,4},{6,5},{7,6},{9,8},{10,9},{11,10},{13,12},{... | collective-permute-start | bytes 98312 | tf_op jit(solution)/shard_map/ppermute | solution.py:17
  126.1 29.9 %copy-start.18 = (f32[65536]{0:T(1024)}, f32[65536]{0:T(1024)S(1)}, u32[]{:S(2)}) copy-start(f32[65536]{0:T(1024)S(1)} %scatter_fusion.7) | copy-start | bytes 786436
Sparse Core Ops, SparseCore 0:
  114.9 30.3 all-gather.1
